TPU v7x, 256 devices: a whole 4x4x8 slice. The times are simulated.
256 devices in a mesh: sec: 4 (over z_hi, core), gx: 16 (over z_lo, y), gy: 4 (over x).
Axes of the slice: x: 4, y: 4, z: 8 (z_hi: 2, z_lo: 4; z = z_hi * 4 + z_lo), core: 2. Of those that a mesh axis runs over, the one named last changes fastest.
Arguments:
- fields: float32 [4, 3, 256, 8192], P('sec', None, 'gx', 'gy'), may hold values from -6 to 6
- x_ops: float32 [4, 3, 256, 256], P(None, None, 'gx'), may hold values from -4 to 4, as said below
- y_ops: float32 [4, 3, 256, 256], P(None, None, 'gy'), may hold values from -4 to 4, as said below
- x_line_class: int32 [256], P('gy'), may hold values from 0 to 3
- y_line_class: int32 [256], P('gx'), may hold values from 0 to 3
- box_offset: int32 [3, 2], replicated, may hold values from 0 to 63, as said below
- coupling: float32 [3, 3, 3], replicated, may hold values from -3 to 3
Outputs:
- fields_next: float32 [4, 3, 256, 8192], P('sec', None, 'gx', 'gy')
Inputs may be any that keep to these rules, and one draw needn't show every extreme that they name: `box_offset`: column 0 is below 16 and column 1 below 64; each column reaches its largest value for some box. `x_ops`: A dense matrix for each class and characteristic. `y_ops`: A dense matrix for each class and characteristic.
All inputs are finite; a program needn't handle non-finite values.
Results may differ from a plain program's by a relative error of at most 0.00013.
Values sent between devices are 32-bit elements; how exact they have to be, the bound alone decides.
A program may use at most 64 MiB of HBM per device.

v0:
```python
import jax
import jax.numpy as jnp
from jax import lax
from jax.sharding import PartitionSpec as P

CZ = 32
NCLASS = 4
STEPS = 2
time_step = 0.2
viscosity = 0.25
highest = lax.Precision.HIGHEST


def padded_2(block, sides, width):
    for axis, dim in sides:
        count = lax.axis_size(axis)
        forward = [(i, i + 1) for i in range(count - 1)]
        backward = [(target, source) for source, target in forward]
        low = lax.ppermute(
            lax.slice_in_dim(block, block.shape[dim] - width, None, axis=dim), axis, forward
        )
        high = lax.ppermute(lax.slice_in_dim(block, 0, width, axis=dim), axis, backward)
        block = jnp.concatenate([low, block, high], axis=dim)
    return block


def shifted(value, axis, steps):
    count = lax.axis_size(axis)
    initial, last = (max(0, -steps), min(count, count - steps))
    return lax.ppermute(value, axis, [(source, source + steps) for source in range(initial, last)])


def flow_core(padded):
    centre = padded[:, 1:-1, 1:-1, :]
    ahead_x = padded[:, 2:, 1:-1, :]
    behind_x = padded[:, :-2, 1:-1, :]
    ahead_y = padded[:, 1:-1, 2:, :]
    behind_y = padded[:, 1:-1, :-2, :]
    ahead_z = jnp.roll(centre, -1, axis=3)
    behind_z = jnp.roll(centre, 1, axis=3)
    slope_x = 0.5 * (ahead_x - behind_x)
    slope_y = 0.5 * (ahead_y - behind_y)
    slope_z = 0.5 * (ahead_z - behind_z)
    laplace = ahead_x + behind_x + ahead_y + behind_y + ahead_z + behind_z - 6.0 * centre
    omega_x = slope_y[2] - slope_z[1]
    omega_y = slope_z[0] - slope_x[2]
    omega_z = slope_x[1] - slope_y[0]
    lamb_vector = jnp.stack(
        [
            omega_y * centre[2] - omega_z * centre[1],
            omega_z * centre[0] - omega_x * centre[2],
            omega_x * centre[1] - omega_y * centre[0],
        ]
    )
    updated = centre + time_step * (viscosity * laplace - lamb_vector)
    return (updated, lamb_vector)


def skip_flow(padded):
    centre = padded[:, 1:-1, 1:-1, :]
    return (centre, jnp.zeros_like(centre))


def unchanged(accrued):
    return accrued


def place_source(padded_lamb, offset_x, offset_y, matrix, span_x, span_y, extent_x, extent_y):
    anchor = jnp.zeros((), jnp.int32)
    corner_x = span_x - offset_x - 1
    corner_y = span_y - offset_y - 1
    window = lax.dynamic_slice(
        padded_lamb,
        (anchor, corner_x, corner_y, anchor),
        (3, extent_x + 1, extent_y + 1, padded_lamb.shape[3]),
    )
    averaged = 0.25 * (
        window[:, :-1, :-1] + window[:, 1:, :-1] + window[:, :-1, 1:] + window[:, 1:, 1:]
    )
    return jnp.einsum("kj,jxyz->kxyz", matrix, averaged, precision=highest)


def sweep_lines_x(state, x_ops, select_x, active):
    initial = jnp.zeros(state.shape[1:], jnp.float32)

    def add_piece(running, portion, anchor):

        def work(accrued):
            partial_value = jnp.einsum("ckij,kjl->ckil", x_ops, portion[0], precision=highest)
            return jnp.sum(partial_value * select_x[:, None, None, :], axis=0)

        return lax.cond(active, work, unchanged, running)

    return add_piece(initial, lax.all_gather(state, "gx", axis=2, tiled=True), jnp.int32(0))


def sweep_lines_y(state, y_ops, select_y, active):
    initial = jnp.zeros(state.shape[1:], jnp.float32)

    def add_piece(running, portion, anchor):

        def work(accrued):
            partial_value = jnp.einsum("ckij,kxjz->ckxiz", y_ops, portion[0], precision=highest)
            return jnp.sum(partial_value * select_y[:, None, :, None, None], axis=0)

        return lax.cond(active, work, unchanged, running)

    return add_piece(initial, lax.all_gather(state, "gy", axis=3, tiled=True), jnp.int32(0))


def local(fields, x_ops, y_ops, x_line_class, y_line_class, box_offset, coupling):
    sections = lax.axis_size("sec")
    section_index = lax.axis_index("sec")
    active = section_index == sections - 1
    member = jnp.minimum(section_index, sections - 2)
    span_x = fields.shape[2]
    merged = fields.shape[3]
    span_y = merged // CZ
    classes = jnp.arange(NCLASS, dtype=jnp.int32)
    select_y = (classes[:, None] == y_line_class[None, :]).astype(jnp.float32)
    offsets = lax.dynamic_index_in_dim(box_offset, member, 0, keepdims=False)
    matrix = lax.dynamic_index_in_dim(coupling, member, 0, keepdims=False)
    current = fields[0].reshape(3, span_x, span_y, CZ)
    for repeat in range(STEPS):
        padded = padded_2(current, (("gx", 1), ("gy", 2)), 1)
        flowed, lamb_vector = lax.cond(active, skip_flow, flow_core, padded)
        left_tile = shifted(lamb_vector, "gx", 1)
        joined = jnp.concatenate([left_tile, lamb_vector], axis=1)
        lower_tile = shifted(joined, "gy", 1)
        joined = jnp.concatenate([lower_tile, joined], axis=2)
        contribution = place_source(
            joined, offsets[0], offsets[1], matrix, span_x, span_y, span_x, span_y
        )
        source = lax.psum(contribution, "sec")
        amplitudes_grid = current + time_step * source
        planes = amplitudes_grid.shape[3]
        merged_now = span_y * planes
        select_x = jnp.broadcast_to(
            (classes[:, None, None] == x_line_class[None, :, None]).astype(jnp.float32),
            (NCLASS, span_y, planes),
        ).reshape(NCLASS, merged_now)
        amplitudes = amplitudes_grid.reshape(1, 3, span_x, merged_now)
        swept_x = sweep_lines_x(amplitudes, x_ops, select_x, active)
        swept = sweep_lines_y(
            swept_x.reshape(1, 3, span_x, span_y, planes), y_ops, select_y, active
        )
        current = jnp.where(active, swept, flowed)
    return current.reshape(1, 3, span_x, merged)


def solution(mesh):
    placed = (
        P("sec", None, "gx", "gy"),
        P(None, None, "gx", None),
        P(None, None, "gy", None),
        P("gy"),
        P("gx"),
        P(),
        P(),
    )
    return jax.shard_map(
        local, mesh=mesh, in_specs=placed, out_specs=P("sec", None, "gx", "gy"), check_vma=False
    )
```

profile of v0, /device:TPU:129, one launch (start us, length us, event | category | flops | bytes accessed | tf_op | source)
XLA Modules:
  0.0 696.2 jit_solution(3194117666119599615)
XLA Ops:
  8.1 3.2 collective-permute-start
  13.1 3.6 collective-permute-done.1
  18.0 4.0 collective-permute-start.2
  31.7 3.4 collective-permute-start.4
  35.1 9.2 %collective-permute-done.4 = f32[3,16,64,32]{2,3,1,0:T(8,128)S(1)} collective-permute-done((f32[3,16,64,32]{2,3,1,0:T(8,128)}, f32[3,16,64,32]{2,3,1,0:T(8,128)S(1)}, u32[]{:S(2)}, u32[]{:S(2)}) %collective-permute-start.4) | collective-permute-done | bytes 393248 | tf_op jit(solution)/shard_map/ppermute | solution.py:30
  44.4 4.3 collective-permute-start.5
  51.9 13.0 %collective-permute-done.5 = f32[3,32,64,32]{2,3,1,0:T(8,128)} collective-permute-done((f32[3,32,64,32]{2,3,1,0:T(8,128)S(1)}, f32[3,32,64,32]{2,3,1,0:T(8,128)}, u32[]{:S(2)}, u32[]{:S(2)}) %collective-permute-start.5) | collective-permute-done | bytes 786464 | tf_op jit(solution)/shard_map/ppermute | solution.py:30
  70.9 97.7 %all-reduce.3.cloned.1.call-done = f32[3,16,64,32]{2,3,1,0:T(8,128)} async-done(((f32[3,16,64,32]{2,3,1,0:T(8,128)}), f32[3,16,64,32]{2,3,1,0:T(8,128)}) %all-reduce.3.cloned.1.call-update) | async-done | bytes 393232 | tf_op jit(solution)/shard_map/psum | solution.py:134
  172.0 83.1 %all-gather.5.cloned.1.call-done = f32[1,3,256,2048]{3,2,1,0:T(8,128)} async-done(((f32[1,3,16,2048]{3,2,1,0:T(8,128)}), f32[1,3,256,2048]{3,2,1,0:T(8,128)}) %all-gather.5.cloned.1.call-update) | async-done | bytes 6291472 | tf_op jit(solution)/shard_map/all_gather | solution.py:94
  255.2 7.1 %conditional.7 = (f32[3,16,2048]{2,1,0:T(8,128)S(1)}) conditional(s32[]{:T(128)} %convert_element_type.20, () %tuple.48, (f32[1,3,256,2048]{3,2,1,0:T(8,128)}, f32[4,3,16,256]{3,2,1,0:T(8,128)S(1)}, f32[4,64,32]{2,1,0:T(8,128)S(1)}) %tuple.131), branch_computations={%region_3.4_spmd, %region_4.6_spmd} | conditional | flops 1208647680 | bytes 6979592 | solution.py:92
  255.4 6.9 fusion.8
  264.2 68.8 %all-gather.7.cloned.1.call-done = f32[1,3,16,256,32]{4,3,2,1,0:T(8,128)} async-done(((f32[1,3,16,64,32]{4,3,2,1,0:T(8,128)}), f32[1,3,16,256,32]{4,3,2,1,0:T(8,128)}) %all-gather.7.cloned.1.call-update) | async-done | bytes 1572880 | tf_op jit(solution)/shard_map/all_gather | solution.py:108
  333.0 21.9 %conditional.8 = (f32[3,16,64,32]{2,3,1,0:T(8,128)S(1)}) conditional(s32[]{:T(128)} %convert_element_type.20, () %tuple.47, (f32[1,3,16,256,32]{4,3,2,1,0:T(8,128)}, f32[4,3,64,256]{3,2,1,0:T(8,128)S(1)}, f32[4,16]{0,1:T(8,128)S(1)}) %tuple.129), branch_computations={%region_6.7_spmd, %region_7.9_spmd} | conditional | flops 1208647680 | bytes 2752776 | solution.py:106
  333.0 21.9 %fusion.14 = f32[3,16,64,32]{2,3,1,0:T(8,128)S(1)} fusion(f32[1,3,16,256,32]{4,3,2,1,0:T(8,128)} %get-tuple-element.138, f32[4,16]{0,1:T(8,128)S(1)} %get-tuple-element.63, f32[4,3,64,256]{3,2,1,0:T(8,128)S(1)} %get-tuple-element.139), kind=kOutput, calls=%fused_computation.22 | convolution fusion | flops 1208647680 | bytes 2752768 | tf_op jit(solution)/shard_map/cond/branch_1_fun/ckij,kxjz->ckxiz/dot_general | solution.py:103
  359.6 3.5 collective-permute-done.7
  378.1 17.3 %collective-permute-done.10 = f32[3,16,64,32]{2,3,1,0:T(8,128)S(1)} collective-permute-done((f32[3,16,64,32]{2,3,1,0:T(8,128)S(1)}, f32[3,16,64,32]{2,3,1,0:T(8,128)S(1)}, u32[]{:S(2)}, u32[]{:S(2)}) %collective-permute-start.10) | collective-permute-done | bytes 393248 | tf_op jit(solution)/shard_map/ppermute | solution.py:30
  398.5 33.3 %collective-permute-done.11 = f32[3,32,64,32]{2,3,1,0:T(8,128)S(1)} collective-permute-done((f32[3,32,64,32]{2,3,1,0:T(8,128)S(1)}, f32[3,32,64,32]{2,3,1,0:T(8,128)S(1)}, u32[]{:S(2)}, u32[]{:S(2)}) %collective-permute-start.11) | collective-permute-done | bytes 786464 | tf_op jit(solution)/shard_map/ppermute | solution.py:30
  436.0 64.7 %all-reduce.5.cloned.1.call-done = f32[3,16,64,32]{2,3,1,0:T(8,128)} async-done(((f32[3,16,64,32]{2,3,1,0:T(8,128)}), f32[3,16,64,32]{2,3,1,0:T(8,128)}) %all-reduce.5.cloned.1.call-update) | async-done | bytes 393232 | tf_op jit(solution)/shard_map/psum | solution.py:134
  504.1 83.2 %all-gather.9.cloned.1.call-done = f32[1,3,256,2048]{3,2,1,0:T(8,128)} async-done(((f32[1,3,16,2048]{3,2,1,0:T(8,128)}), f32[1,3,256,2048]{3,2,1,0:T(8,128)}) %all-gather.9.cloned.1.call-update) | async-done | bytes 6291472 | tf_op jit(solution)/shard_map/all_gather | solution.py:94
  587.2 7.2 %conditional.10 = (f32[3,16,2048]{2,1,0:T(8,128)S(1)}) conditional(s32[]{:T(128)} %convert_element_type.20, () %tuple.46, (f32[1,3,256,2048]{3,2,1,0:T(8,128)}, f32[4,3,16,256]{3,2,1,0:T(8,128)S(1)}, f32[4,64,32]{2,1,0:T(8,128)S(1)}) %tuple.132), branch_computations={%region_12.13_spmd, %region_13.15_spmd} | conditional | flops 1208647680 | bytes 6979592 | solution.py:92
  587.5 6.9 fusion.26
  596.2 68.9 %all-gather.11.cloned.1.call-done = f32[1,3,16,256,32]{4,3,2,1,0:T(8,128)} async-done(((f32[1,3,16,64,32]{4,3,2,1,0:T(8,128)}), f32[1,3,16,256,32]{4,3,2,1,0:T(8,128)}) %all-gather.11.cloned.1.call-update) | async-done | bytes 1572880 | tf_op jit(solution)/shard_map/all_gather | solution.py:108
  665.1 21.9 %conditional.11 = (f32[3,16,64,32]{2,3,1,0:T(8,128)S(1)}) conditional(s32[]{:T(128)} %convert_element_type.20, () %tuple.45, (f32[1,3,16,256,32]{4,3,2,1,0:T(8,128)}, f32[4,3,64,256]{3,2,1,0:T(8,128)S(1)}, f32[4,16]{0,1:T(8,128)S(1)}) %tuple.130), branch_computations={%region_15.16_spmd, %region_16.18_spmd} | conditional | flops 1208647680 | bytes 2752776 | solution.py:106
  665.1 21.9 %fusion.32 = f32[3,16,64,32]{2,3,1,0:T(8,128)S(1)} fusion(f32[1,3,16,256,32]{4,3,2,1,0:T(8,128)} %get-tuple-element.147, f32[4,16]{0,1:T(8,128)S(1)} %get-tuple-element.72, f32[4,3,64,256]{3,2,1,0:T(8,128)S(1)} %get-tuple-element.148), kind=kOutput, calls=%fused_computation.46 | convolution fusion | flops 1208647680 | bytes 2752768 | tf_op jit(solution)/shard_map/cond/branch_1_fun/ckij,kxjz->ckxiz/dot_general | solution.py:103
  (108 shorter events, 63.2 us)
Async XLA Ops:
  6.5 60.5 %copy-start = (f32[3,3,3]{2,1,0:T(4,128)S(1)}, f32[3,3,3]{2,1,0:T(4,128)}, u32[]{:S(2)}) copy-start(f32[3,3,3]{2,1,0:T(4,128)} %param.25) | copy-start | bytes 328
  6.5 162.0 %all-reduce.3.cloned.1.call-start = ((), (), s32[]{:S(2)}) async-start(), calls=%async_computation | async-start | bytes 1572864 | tf_op jit(solution)/shard_map/psum | solution.py:134
  8.1 4.8 collective-permute-start
  11.3 5.4 collective-permute-start.1
  16.7 6.7 collective-permute-start.3
  18.0 6.8 collective-permute-start.2
  31.7 12.6 %collective-permute-start.4 = (f32[3,16,64,32]{2,3,1,0:T(8,128)}, f32[3,16,64,32]{2,3,1,0:T(8,128)S(1)}, u32[]{:S(2)}, u32[]{:S(2)}) collective-permute-start(f32[3,16,64,32]{2,3,1,0:T(8,128)} %get-tuple-element.150), channel_id=1, source_target_pairs={{0,4},{4,8},{8,12},{12,16},{16,20},{20,24},{24,28},{28,32},{32,36}... | collective-permute-start | bytes 1179656 | tf_op jit(solution)/shard_map/ppermute | solution.py:30
  44.4 20.5 %collective-permute-start.5 = (f32[3,32,64,32]{2,3,1,0:T(8,128)S(1)}, f32[3,32,64,32]{2,3,1,0:T(8,128)}, u32[]{:S(2)}, u32[]{:S(2)}) collective-permute-start(f32[3,32,64,32]{2,3,1,0:T(8,128)S(1)} %constant_dynamic-update-slice_fusion.3), channel_id=1, source_target_pairs={{0,1},{1,2},{2,3},{4,5},{5,6},{6,7},{8,9},{9,10},{10,11},{12,13},{... | collective-permute-start | bytes 2359304 | tf_op jit(solution)/shard_map/ppermute | solution.py:30
  70.2 184.9 %all-gather.5.cloned.1.call-start = ((), (), s32[]{:S(2)}) async-start(), calls=%async_computation.1 | async-start | bytes 6684672 | tf_op jit(solution)/shard_map/all_gather | solution.py:94
  170.4 84.8 %copy-start.12 = (f32[4,3,16,256]{3,2,1,0:T(8,128)S(1)}, f32[4,3,16,256]{3,2,1,0:T(8,128)}, u32[]{:S(2)}) copy-start(f32[4,3,16,256]{3,2,1,0:T(8,128)} %param.20) | copy-start | bytes 589828
  171.9 161.1 %all-gather.7.cloned.1.call-start = ((), (), s32[]{:S(2)}) async-start(), calls=%async_computation.2 | async-start | bytes 7864320 | tf_op jit(solution)/shard_map/all_gather | solution.py:108
  262.3 70.7 %copy-start.8 = (f32[4,3,64,256]{3,2,1,0:T(8,128)S(1)}, f32[4,3,64,256]{3,2,1,0:T(8,128)}, u32[]{:S(2)}) copy-start(f32[4,3,64,256]{3,2,1,0:T(8,128)} %param.21) | copy-start | bytes 2359300
  264.1 236.6 %all-reduce.5.cloned.1.call-start = ((), (), s32[]{:S(2)}) async-start(), calls=%async_computation.3 | async-start | bytes 1572864 | tf_op jit(solution)/shard_map/psum | solution.py:134
  355.1 4.4 collective-permute-start.6
  358.2 4.8 collective-permute-start.7
  364.8 4.5 collective-permute-start.8
  368.0 4.6 collective-permute-start.9
  375.0 20.5 %collective-permute-start.10 = (f32[3,16,64,32]{2,3,1,0:T(8,128)S(1)}, f32[3,16,64,32]{2,3,1,0:T(8,128)S(1)}, u32[]{:S(2)}, u32[]{:S(2)}) collective-permute-start(f32[3,16,64,32]{2,3,1,0:T(8,128)S(1)} %get-tuple-element.152), channel_id=1, source_target_pairs={{0,4},{4,8},{8,12},{12,16},{16,20},{20,24},{24,28},{28,32},{32,36}... | collective-permute-start | bytes 1179656 | tf_op jit(solution)/shard_map/ppermute | solution.py:30
  395.6 36.2 %collective-permute-start.11 = (f32[3,32,64,32]{2,3,1,0:T(8,128)S(1)}, f32[3,32,64,32]{2,3,1,0:T(8,128)S(1)}, u32[]{:S(2)}, u32[]{:S(2)}) collective-permute-start(f32[3,32,64,32]{2,3,1,0:T(8,128)S(1)} %constant_dynamic-update-slice_fusion.5), channel_id=1, source_target_pairs={{0,1},{1,2},{2,3},{4,5},{5,6},{6,7},{8,9},{9,10},{10,11},{12,13},{... | collective-permute-start | bytes 2359304 | tf_op jit(solution)/shard_map/ppermute | solution.py:30
  435.0 65.7 %copy-start.4 = (f32[3,16,64,32]{2,3,1,0:T(8,128)S(1)}, f32[3,16,64,32]{2,3,1,0:T(8,128)}, u32[]{:S(2)}) copy-start(f32[3,16,64,32]{2,3,1,0:T(8,128)} %copy-done.3) | copy-start | bytes 1179652
  436.0 151.2 %all-gather.9.cloned.1.call-start = ((), (), s32[]{:S(2)}) async-start(), calls=%async_computation.4 | async-start | bytes 6684672 | tf_op jit(solution)/shard_map/all_gather | solution.py:94
  502.5 84.7 %copy-start.13 = (f32[4,3,16,256]{3,2,1,0:T(8,128)S(1)}, f32[4,3,16,256]{3,2,1,0:T(8,128)}, u32[]{:S(2)}) copy-start(f32[4,3,16,256]{3,2,1,0:T(8,128)} %param.20) | copy-start | bytes 589828
  504.0 161.1 %all-gather.11.cloned.1.call-start = ((), (), s32[]{:S(2)}) async-start(), calls=%async_computation.5 | async-start | bytes 7864320 | tf_op jit(solution)/shard_map/all_gather | solution.py:108
  594.4 70.7 %copy-start.9 = (f32[4,3,64,256]{3,2,1,0:T(8,128)S(1)}, f32[4,3,64,256]{3,2,1,0:T(8,128)}, u32[]{:S(2)}) copy-start(f32[4,3,64,256]{3,2,1,0:T(8,128)} %param.21) | copy-start | bytes 2359300
  (7 other events, 75.2 us)
Sparse Core Ops, SparseCore 0:
  70.4 98.1 all-reduce.2
  172.0 83.0 all-gather.4
  264.2 68.7 all-gather.6
  436.1 64.5 all-reduce.4
  504.1 83.0 all-gather.8
  596.3 68.7 all-gather.10
where the time goes:
time: 705 us; the launch traced here: 696 us
  waiting for transfers between devices  549 us (78%)
  matrix products  62.1 us (9%)
  starting transfers between devices  32.4 us (5%)
  local copies, waits for them, and re-layouts  24.3 us (3%)
  between operations  16.6 us (2%)
  other arithmetic  10.8 us (2%)
    all_gather x2, waiting for transfers between devices, sweep_lines_x(): lax.all_gather(state, 'gx', axis=2, tiled=True)  166 us
    psum x2, waiting for transfers between devices, local(): source = lax.psum(contribution, 'sec')  162 us
    all_gather x2, waiting for transfers between devices, sweep_lines_y(): lax.all_gather(state, 'gy', axis=3, tiled=True)  138 us
    ppermute x4, waiting for transfers between devices, shifted(): lax.ppermute(value, axis, [(source, source + steps) for source in range(i...  72.8 us
    dot_general x2, matrix products, work(): jnp.einsum('ckij,kxjz->ckxiz', y_ops, portion[0], precision=highest)  43.8 us
  transfers between devices with their start and end apart: 18, of which 14 were waited for; matrix products, arithmetic and copies ran while one was open for 1% of the time, Pallas kernels for 0%

commit v1 on v0

--- a/solution.py
+++ b/solution.py
@@ -91,7 +91,13 @@
 
         return lax.cond(active, work, unchanged, running)
 
-    return add_piece(initial, lax.all_gather(state, "gx", axis=2, tiled=True), jnp.int32(0))
+    return add_piece(
+        initial,
+        jnp.concatenate(
+            lax.all_to_all(jnp.stack([state] * lax.axis_size("gx")), "gx", 0, 0), axis=2
+        ),
+        jnp.int32(0),
+    )
 
 
 def sweep_lines_y(state, y_ops, select_y, active):

time: 705 us -> 829 us (1.18)
  waiting for transfers between devices: 549 us -> 659 us
  local copies, waits for them, and re-layouts: 24.3 us -> 35.7 us
  starting transfers between devices: 32.4 us -> 43 us
    all_to_all x0 -> x2, waiting for transfers between devices: none -> 231 us  [sweep_lines_x(): lax.all_to_all(jnp.stack([state] * lax.axis_size('gx')), 'gx', 0, 0)]
    all_gather x2 -> x0, waiting for transfers between devices: 166 us -> none  [sweep_lines_x(): lax.all_gather(state, 'gx', axis=2, tiled=True)]
    all_gather x2, waiting for transfers between devices: 138 us -> 183 us  [sweep_lines_y(): lax.all_gather(state, 'gy', axis=3, tiled=True)]
    another operation x2 -> x8, local copies, waits for them, and re-layouts: 1.09 us -> 15.9 us  [the longest x4 8.42 us: sweep_lines_x(): jnp.stack([state] * lax.axis_size('gx'))]
    all_to_all x0 -> x2, starting transfers between devices: none -> 10.7 us  [sweep_lines_x(): lax.all_to_all(jnp.stack([state] * lax.axis_size('gx')), 'gx', 0, 0)]
where the time goes in v1:
time: 829 us; the launch traced here: 822 us
  waiting for transfers between devices  659 us (79%)
  matrix products  56.6 us (7%)
  starting transfers between devices  43 us (5%)
  local copies, waits for them, and re-layouts  35.7 us (4%)
  between operations  16.3 us (2%)
  other arithmetic  10.8 us (1%)
    all_to_all x2, waiting for transfers between devices, sweep_lines_x(): lax.all_to_all(jnp.stack([state] * lax.axis_size('gx')), 'gx', 0, 0)  231 us
    all_gather x2, waiting for transfers between devices, sweep_lines_y(): lax.all_gather(state, 'gy', axis=3, tiled=True)  183 us
    psum x2, waiting for transfers between devices, local(): source = lax.psum(contribution, 'sec')  162 us
    ppermute x4, waiting for transfers between devices, shifted(): lax.ppermute(value, axis, [(source, source + steps) for source in range(i...  72.5 us
    dot_general x2, matrix products, work(): jnp.einsum('ckij,kxjz->ckxiz', y_ops, portion[0], precision=highest)  43.8 us
  transfers between devices with their start and end apart: 18, of which 14 were waited for; matrix products, arithmetic and copies ran while one was open for 1% of the time, Pallas kernels for 0%

profile of v1, /device:TPU:129, one launch (start us, length us, event | category | flops | bytes accessed | tf_op | source)
XLA Modules:
  0.0 822.2 jit_solution(6178038010264980018)
XLA Ops:
  13.1 3.6 collective-permute-done.1
  18.0 4.0 collective-permute-start.2
  35.0 9.2 %collective-permute-done.4 = f32[3,16,64,32]{2,3,1,0:T(8,128)S(1)} collective-permute-done((f32[3,16,64,32]{2,3,1,0:T(8,128)}, f32[3,16,64,32]{2,3,1,0:T(8,128)S(1)}, u32[]{:S(2)}, u32[]{:S(2)}) %collective-permute-start.4) | collective-permute-done | bytes 393248 | tf_op jit(solution)/shard_map/ppermute | solution.py:30
  44.3 4.4 collective-permute-start.5
  51.9 12.8 %collective-permute-done.5 = f32[3,32,64,32]{2,3,1,0:T(8,128)} collective-permute-done((f32[3,32,64,32]{2,3,1,0:T(8,128)S(1)}, f32[3,32,64,32]{2,3,1,0:T(8,128)}, u32[]{:S(2)}, u32[]{:S(2)}) %collective-permute-start.5) | collective-permute-done | bytes 786464 | tf_op jit(solution)/shard_map/ppermute | solution.py:30
  70.6 97.9 %all-reduce.3.cloned.1.call-done = f32[3,16,64,32]{2,3,1,0:T(8,128)} async-done(((f32[3,16,64,32]{2,3,1,0:T(8,128)}), f32[3,16,64,32]{2,3,1,0:T(8,128)}) %all-reduce.3.cloned.1.call-update) | async-done | bytes 393232 | tf_op jit(solution)/shard_map/psum | solution.py:140
  174.5 5.3 all-to-all-start
  179.9 115.3 %all-to-all-done = f32[16,1,3,16,2048]{4,3,2,1,0:T(8,128)} async-done(((f32[16,1,3,16,2048]{4,3,2,1,0:T(8,128)}), f32[16,1,3,16,2048]{4,3,2,1,0:T(8,128)}, u32[]{:S(2)}, u32[]{:S(2)}) %all-to-all-start) | async-done | bytes 6291488 | tf_op jit(solution)/shard_map/all_to_all | solution.py:97
  295.3 7.6 conditional.7
  298.7 4.2 fusion.1
  304.8 91.5 %all-gather.3.cloned.1.call-done = f32[1,3,16,256,32]{4,3,2,1,0:T(8,128)} async-done(((f32[1,3,16,64,32]{4,3,2,1,0:T(8,128)}), f32[1,3,16,256,32]{4,3,2,1,0:T(8,128)}) %all-gather.3.cloned.1.call-update) | async-done | bytes 1572880 | tf_op jit(solution)/shard_map/all_gather | solution.py:114
  396.3 22.1 %conditional.8 = (f32[3,16,64,32]{2,3,1,0:T(8,128)S(1)}) conditional(s32[]{:T(128)} %convert_element_type.20, () %tuple.47, (f32[1,3,16,256,32]{4,3,2,1,0:T(8,128)}, f32[4,3,64,256]{3,2,1,0:T(8,128)S(1)}, f32[4,16]{0,1:T(8,128)S(1)}) %tuple.125), branch_computations={%region_6.7_spmd, %region_7.9_spmd} | conditional | flops 1208647680 | bytes 2752776 | solution.py:112
  396.5 21.9 %fusion.5 = f32[3,16,64,32]{2,3,1,0:T(8,128)S(1)} fusion(f32[1,3,16,256,32]{4,3,2,1,0:T(8,128)} %get-tuple-element.138, f32[4,16]{0,1:T(8,128)S(1)} %get-tuple-element.63, f32[4,3,64,256]{3,2,1,0:T(8,128)S(1)} %get-tuple-element.139), kind=kOutput, calls=%fused_computation.20 | convolution fusion | flops 1208647680 | bytes 2752768 | tf_op jit(solution)/shard_map/cond/branch_1_fun/ckij,kxjz->ckxiz/dot_general | solution.py:109
  423.0 3.5 collective-permute-done.7
  441.3 17.1 %collective-permute-done.10 = f32[3,16,64,32]{2,3,1,0:T(8,128)S(1)} collective-permute-done((f32[3,16,64,32]{2,3,1,0:T(8,128)S(1)}, f32[3,16,64,32]{2,3,1,0:T(8,128)S(1)}, u32[]{:S(2)}, u32[]{:S(2)}) %collective-permute-start.10) | collective-permute-done | bytes 393248 | tf_op jit(solution)/shard_map/ppermute | solution.py:30
  461.4 33.5 %collective-permute-done.11 = f32[3,32,64,32]{2,3,1,0:T(8,128)S(1)} collective-permute-done((f32[3,32,64,32]{2,3,1,0:T(8,128)S(1)}, f32[3,32,64,32]{2,3,1,0:T(8,128)S(1)}, u32[]{:S(2)}, u32[]{:S(2)}) %collective-permute-start.11) | collective-permute-done | bytes 786464 | tf_op jit(solution)/shard_map/ppermute | solution.py:30
  499.1 64.5 %all-reduce.5.cloned.1.call-done = f32[3,16,64,32]{2,3,1,0:T(8,128)} async-done(((f32[3,16,64,32]{2,3,1,0:T(8,128)}), f32[3,16,64,32]{2,3,1,0:T(8,128)}) %all-reduce.5.cloned.1.call-update) | async-done | bytes 393232 | tf_op jit(solution)/shard_map/psum | solution.py:140
  569.6 5.3 all-to-all-start.1
  575.0 115.3 %all-to-all-done.1 = f32[16,1,3,16,2048]{4,3,2,1,0:T(8,128)} async-done(((f32[16,1,3,16,2048]{4,3,2,1,0:T(8,128)}), f32[16,1,3,16,2048]{4,3,2,1,0:T(8,128)}, u32[]{:S(2)}, u32[]{:S(2)}) %all-to-all-start.1) | async-done | bytes 6291488 | tf_op jit(solution)/shard_map/all_to_all | solution.py:97
  690.3 7.7 conditional.10
  693.8 4.2 fusion.10
  699.8 91.6 %all-gather.5.cloned.1.call-done = f32[1,3,16,256,32]{4,3,2,1,0:T(8,128)} async-done(((f32[1,3,16,64,32]{4,3,2,1,0:T(8,128)}), f32[1,3,16,256,32]{4,3,2,1,0:T(8,128)}) %all-gather.5.cloned.1.call-update) | async-done | bytes 1572880 | tf_op jit(solution)/shard_map/all_gather | solution.py:114
  791.4 21.9 %conditional.11 = (f32[3,16,64,32]{2,3,1,0:T(8,128)S(1)}) conditional(s32[]{:T(128)} %convert_element_type.20, () %tuple.45, (f32[1,3,16,256,32]{4,3,2,1,0:T(8,128)}, f32[4,3,64,256]{3,2,1,0:T(8,128)S(1)}, f32[4,16]{0,1:T(8,128)S(1)}) %tuple.126), branch_computations={%region_15.16_spmd, %region_16.18_spmd} | conditional | flops 1208647680 | bytes 2752776 | solution.py:112
  791.4 21.9 %fusion.14 = f32[3,16,64,32]{2,3,1,0:T(8,128)S(1)} fusion(f32[1,3,16,256,32]{4,3,2,1,0:T(8,128)} %get-tuple-element.147, f32[4,16]{0,1:T(8,128)S(1)} %get-tuple-element.72, f32[4,3,64,256]{3,2,1,0:T(8,128)S(1)} %get-tuple-element.148), kind=kOutput, calls=%fused_computation.42 | convolution fusion | flops 1208647680 | bytes 2752768 | tf_op jit(solution)/shard_map/cond/branch_1_fun/ckij,kxjz->ckxiz/dot_general | solution.py:109
  (110 shorter events, 80.8 us)
Async XLA Ops:
  6.5 60.4 %copy-start = (f32[3,3,3]{2,1,0:T(4,128)S(1)}, f32[3,3,3]{2,1,0:T(4,128)}, u32[]{:S(2)}) copy-start(f32[3,3,3]{2,1,0:T(4,128)} %param.25) | copy-start | bytes 328
  6.5 161.9 %all-reduce.3.cloned.1.call-start = ((), (), s32[]{:S(2)}) async-start(), calls=%async_computation.2 | async-start | bytes 1572864 | tf_op jit(solution)/shard_map/psum | solution.py:140
  8.1 4.8 collective-permute-start
  11.3 5.4 collective-permute-start.1
  16.7 6.7 collective-permute-start.3
  18.0 6.8 collective-permute-start.2
  31.6 12.6 %collective-permute-start.4 = (f32[3,16,64,32]{2,3,1,0:T(8,128)}, f32[3,16,64,32]{2,3,1,0:T(8,128)S(1)}, u32[]{:S(2)}, u32[]{:S(2)}) collective-permute-start(f32[3,16,64,32]{2,3,1,0:T(8,128)} %get-tuple-element.150), channel_id=1, source_target_pairs={{0,4},{4,8},{8,12},{12,16},{16,20},{20,24},{24,28},{28,32},{32,36}... | collective-permute-start | bytes 1179656 | tf_op jit(solution)/shard_map/ppermute | solution.py:30
  44.3 20.5 %collective-permute-start.5 = (f32[3,32,64,32]{2,3,1,0:T(8,128)S(1)}, f32[3,32,64,32]{2,3,1,0:T(8,128)}, u32[]{:S(2)}, u32[]{:S(2)}) collective-permute-start(f32[3,32,64,32]{2,3,1,0:T(8,128)S(1)} %constant_dynamic-update-slice_fusion.3), channel_id=1, source_target_pairs={{0,1},{1,2},{2,3},{4,5},{5,6},{6,7},{8,9},{9,10},{10,11},{12,13},{... | collective-permute-start | bytes 2359304 | tf_op jit(solution)/shard_map/ppermute | solution.py:30
  174.5 120.8 %copy-start.12 = (f32[4,3,16,256]{3,2,1,0:T(8,128)S(1)}, f32[4,3,16,256]{3,2,1,0:T(8,128)}, u32[]{:S(2)}) copy-start(f32[4,3,16,256]{3,2,1,0:T(8,128)} %param.20) | copy-start | bytes 589828
  174.5 120.7 %all-to-all-start = ((f32[16,1,3,16,2048]{4,3,2,1,0:T(8,128)}), f32[16,1,3,16,2048]{4,3,2,1,0:T(8,128)}, u32[]{:S(2)}, u32[]{:S(2)}) async-start(f32[16,1,3,16,2048]{4,3,2,1,0:T(8,128)} %stack.12), calls=%async_computation | async-start | bytes 12582912 | tf_op jit(solution)/shard_map/all_to_all | solution.py:97
  179.8 216.5 %all-gather.3.cloned.1.call-start = ((), (), s32[]{:S(2)}) async-start(), calls=%async_computation.3 | async-start | bytes 7864320 | tf_op jit(solution)/shard_map/all_gather | solution.py:114
  302.9 93.4 %copy-start.8 = (f32[4,3,64,256]{3,2,1,0:T(8,128)S(1)}, f32[4,3,64,256]{3,2,1,0:T(8,128)}, u32[]{:S(2)}) copy-start(f32[4,3,64,256]{3,2,1,0:T(8,128)} %param.21) | copy-start | bytes 2359300
  304.7 258.9 %all-reduce.5.cloned.1.call-start = ((), (), s32[]{:S(2)}) async-start(), calls=%async_computation.4 | async-start | bytes 1572864 | tf_op jit(solution)/shard_map/psum | solution.py:140
  418.6 4.4 collective-permute-start.6
  421.7 4.8 collective-permute-start.7
  427.9 4.5 collective-permute-start.8
  431.1 4.6 collective-permute-start.9
  438.1 20.2 %collective-permute-start.10 = (f32[3,16,64,32]{2,3,1,0:T(8,128)S(1)}, f32[3,16,64,32]{2,3,1,0:T(8,128)S(1)}, u32[]{:S(2)}, u32[]{:S(2)}) collective-permute-start(f32[3,16,64,32]{2,3,1,0:T(8,128)S(1)} %get-tuple-element.152), channel_id=1, source_target_pairs={{0,4},{4,8},{8,12},{12,16},{16,20},{20,24},{24,28},{28,32},{32,36}... | collective-permute-start | bytes 1179656 | tf_op jit(solution)/shard_map/ppermute | solution.py:30
  458.5 36.4 %collective-permute-start.11 = (f32[3,32,64,32]{2,3,1,0:T(8,128)S(1)}, f32[3,32,64,32]{2,3,1,0:T(8,128)S(1)}, u32[]{:S(2)}, u32[]{:S(2)}) collective-permute-start(f32[3,32,64,32]{2,3,1,0:T(8,128)S(1)} %constant_dynamic-update-slice_fusion.5), channel_id=1, source_target_pairs={{0,1},{1,2},{2,3},{4,5},{5,6},{6,7},{8,9},{9,10},{10,11},{12,13},{... | collective-permute-start | bytes 2359304 | tf_op jit(solution)/shard_map/ppermute | solution.py:30
  498.0 65.5 %copy-start.4 = (f32[3,16,64,32]{2,3,1,0:T(8,128)S(1)}, f32[3,16,64,32]{2,3,1,0:T(8,128)}, u32[]{:S(2)}) copy-start(f32[3,16,64,32]{2,3,1,0:T(8,128)} %copy-done.3) | copy-start | bytes 1179652
  569.6 120.7 %copy-start.13 = (f32[4,3,16,256]{3,2,1,0:T(8,128)S(1)}, f32[4,3,16,256]{3,2,1,0:T(8,128)}, u32[]{:S(2)}) copy-start(f32[4,3,16,256]{3,2,1,0:T(8,128)} %param.20) | copy-start | bytes 589828
  569.6 120.7 %all-to-all-start.1 = ((f32[16,1,3,16,2048]{4,3,2,1,0:T(8,128)}), f32[16,1,3,16,2048]{4,3,2,1,0:T(8,128)}, u32[]{:S(2)}, u32[]{:S(2)}) async-start(f32[16,1,3,16,2048]{4,3,2,1,0:T(8,128)} %stack.17), calls=%async_computation.1 | async-start | bytes 12582912 | tf_op jit(solution)/shard_map/all_to_all | solution.py:97
  574.9 216.5 %all-gather.5.cloned.1.call-start = ((), (), s32[]{:S(2)}) async-start(), calls=%async_computation.5 | async-start | bytes 7864320 | tf_op jit(solution)/shard_map/all_gather | solution.py:114
  698.0 93.4 %copy-start.9 = (f32[4,3,64,256]{3,2,1,0:T(8,128)S(1)}, f32[4,3,64,256]{3,2,1,0:T(8,128)}, u32[]{:S(2)}) copy-start(f32[4,3,64,256]{3,2,1,0:T(8,128)} %param.21) | copy-start | bytes 2359300
  (7 other events, 79.0 us)
Sparse Core Ops, SparseCore 0:
  70.2 98.1 all-reduce.2
  304.8 91.4 all-gather.2
  499.2 64.3 all-reduce.4
  699.9 91.4 all-gather.4
